TPU v7x, 32 devices: a whole 2x2x4 slice. The times are simulated.
32 devices in a mesh: expert: 4 (over y, core), dp: 8 (over z, x).
Axes of the slice: x: 2, y: 2, z: 4, core: 2. Of those that a mesh axis runs over, the one named last changes fastest.
Arguments:
- tokens: bfloat16 [4096, 1024], P(('expert', 'dp')), may hold values from -6 to 6
- d_output: bfloat16 [4096, 1024], P(('expert', 'dp')), may hold values from -6 to 6
- expert_ids: int32 [4096, 8], P(('expert', 'dp')), may hold values from 0 to 127, as said below
- gate_scores: bfloat16 [4096, 8], P(('expert', 'dp')), may hold values from 0.099609375 to 1
- gate_up_w: bfloat16 [4, 1024, 768], P('expert', 'dp'), may hold values from -0.1875 to 0.1875
- down_w: bfloat16 [4, 1024, 384], P('expert', 'dp'), may hold values from -0.3125 to 0.3125
Outputs:
- d_tokens: bfloat16 [4096, 1024], P(('expert', 'dp'))
- d_gates: bfloat16 [4096, 8], P(('expert', 'dp'))
- d_down: float32 [4, 1024, 384], P('expert', 'dp')
Inputs may be any that keep to these rules, and one draw needn't show every extreme that they name: `expert_ids`: each token names 8 different experts. The tokens of one device name no expert more than 12 times, and in every draw one expert below 4 is named exactly 12 times by the tokens of every device.
All inputs are finite; a program needn't handle non-finite values.
Results may differ from a plain program's by a relative error of at most 0.0062.
Values may be sent and summed in bfloat16 or wider, within the bound.
A program may use at most 64 MiB of HBM per device.

v0:
```python
import jax
import jax.numpy as jnp
from jax import lax
from jax.sharding import PartitionSpec as P

TOPK = 8
CAP = 12


def transpose_product(left, right):
    return lax.dot_general(
        left, right, (((0,), (0,)), ((), ())), preferred_element_type=jnp.float32
    )


def product_transposed(left, right):
    return lax.dot_general(
        left, right, (((1,), (1,)), ((), ())), preferred_element_type=jnp.float32
    )


def on_device(tokens, d_output, expert_ids, gate_scores, gate_up_w, down_w):
    gate_full, down_full = (
        lax.all_gather(gate_up_w, "dp", axis=1, tiled=True),
        lax.all_gather(down_w, "dp", axis=1, tiled=True),
    )
    gate_full = gate_full[0]
    down_full = down_full[0]
    groups = lax.axis_size("expert")
    slot_count = groups * CAP
    tok_rows = tokens.shape[0]
    features = tokens.shape[1]
    width = down_w.shape[2]
    flat_ids = expert_ids.reshape(-1)
    entries = flat_ids.shape[0]
    one_hot = (flat_ids[:, None] == jnp.arange(groups, dtype=jnp.int32)[None, :]).astype(jnp.int32)
    earlier = jnp.cumsum(one_hot, axis=0) - one_hot
    within = jnp.sum(earlier * one_hot, axis=1)
    inside = flat_ids < groups
    slot_of = jnp.where(inside, flat_ids * CAP + within, slot_count)
    owner = (
        jnp.full((slot_count,), -1, jnp.int32)
        .at[slot_of]
        .set(jnp.arange(entries, dtype=jnp.int32), mode="drop")
    )
    filled = owner >= 0
    source = jnp.maximum(owner, 0)
    token_of = jnp.where(filled, source // TOPK, -1)
    picker = (token_of[:, None] == jnp.arange(tok_rows, dtype=jnp.int32)[None, :]).astype(
        jnp.bfloat16
    )
    send_inputs = jnp.dot(picker, tokens, preferred_element_type=jnp.float32).astype(jnp.bfloat16)
    send_upstream = jnp.dot(picker, d_output, preferred_element_type=jnp.float32).astype(
        jnp.bfloat16
    )
    send_gates = jnp.where(filled, gate_scores.reshape(-1)[source], jnp.zeros((), jnp.bfloat16))
    recv_inputs, recv_upstream, recv_gates = (
        lax.all_to_all(
            send_inputs.reshape(groups, CAP, features),
            "expert",
            split_axis=0,
            concat_axis=0,
            tiled=True,
        ),
        lax.all_to_all(
            send_upstream.reshape(groups, CAP, features),
            "expert",
            split_axis=0,
            concat_axis=0,
            tiled=True,
        ),
        lax.all_to_all(
            send_gates.reshape(groups, CAP), "expert", split_axis=0, concat_axis=0, tiled=True
        ),
    )
    slot_inputs = recv_inputs.reshape(slot_count, features)
    slot_upstream = recv_upstream.reshape(slot_count, features)
    slot_gates = recv_gates.reshape(slot_count).astype(jnp.float32)
    pre_act = jnp.dot(slot_inputs, gate_full, preferred_element_type=jnp.float32)
    gate_part = pre_act[:, :width]
    up_part = pre_act[:, width:]
    sigma = jax.nn.sigmoid(gate_part)
    activ = gate_part * sigma
    hidden = (activ * up_part).astype(jnp.bfloat16)
    expert_out = product_transposed(hidden, down_full)
    upstream_float = slot_upstream.astype(jnp.float32)
    slot_grad = jnp.sum(upstream_float * expert_out, axis=1).astype(jnp.bfloat16)
    d_expert_out = (slot_gates[:, None] * upstream_float).astype(jnp.bfloat16)
    d_hidden = jnp.dot(d_expert_out, down_full, preferred_element_type=jnp.float32)
    d_gate_part = d_hidden * up_part * sigma * (1.0 + gate_part * (1.0 - sigma))
    d_up_part = d_hidden * activ
    d_pre = jnp.concatenate([d_gate_part, d_up_part], axis=1).astype(jnp.bfloat16)
    d_slot = product_transposed(d_pre, gate_full).astype(jnp.bfloat16)
    down_share = lax.psum_scatter(
        transpose_product(d_expert_out, hidden), "dp", scatter_dimension=0, tiled=True
    )
    back_rows, back_grads = (
        lax.all_to_all(
            d_slot.reshape(groups, CAP, features), "expert", split_axis=0, concat_axis=0, tiled=True
        ),
        lax.all_to_all(
            slot_grad.reshape(groups, CAP), "expert", split_axis=0, concat_axis=0, tiled=True
        ),
    )
    back_rows = back_rows.reshape(slot_count, features)
    back_grads = back_grads.reshape(slot_count)
    grad_tokens = transpose_product(picker, back_rows).astype(jnp.bfloat16)
    gathered_grads = back_grads[jnp.minimum(slot_of, slot_count - 1)]
    grad_gates = jnp.where(inside, gathered_grads, jnp.zeros((), jnp.bfloat16)).reshape(
        tok_rows, TOPK
    )
    return (grad_tokens, grad_gates, down_share[None])


def solution(mesh):
    return jax.shard_map(
        on_device,
        mesh=mesh,
        in_specs=(
            P(("expert", "dp"), None),
            P(("expert", "dp"), None),
            P(("expert", "dp"), None),
            P(("expert", "dp"), None),
            P("expert", "dp", None),
            P("expert", "dp", None),
        ),
        out_specs=(P(("expert", "dp"), None), P(("expert", "dp"), None), P("expert", "dp", None)),
        check_vma=False,
    )
```

profile of v0, /device:TPU:0, one launch (start us, length us, event | category | flops | bytes accessed | tf_op | source)
XLA Modules:
  0.0 151.1 jit_solution(2846326151058442494)
XLA Ops:
  7.9 0.8 copy.23
  8.8 1.1 reduce-window.6
  10.6 0.7 broadcast_multiply_fusion
  11.5 0.8 copy.27
  12.5 4.3 %scatter_custom_fusion = s32[48]{0:T(128)S(1)} fusion(s32[1024]{0:T(1024)S(1)} %bitcast.96, s32[1024]{0:T(1024)S(1)} %iota.15, s32[]{:T(128)} %constant.14.clone.1), kind=kCustom, calls=%fused_computation.100 | custom fusion | bytes 196 | tf_op jit(solution)/shard_map/scatter | solution.py:44
  16.9 0.8 gather_fusion
  18.3 4.3 %all-to-all-start = ((bf16[4,1,12]{2,1,0:T(2,128)(2,1)}), bf16[4,1,12]{2,1,0:T(2,128)(2,1)S(1)}, u32[]{:S(2)}, u32[]{:S(2)}) async-start(bf16[4,1,12]{2,1,0:T(2,128)(2,1)} %all_to_all.25), calls=%async_computation | async-start | bytes 4096 | tf_op jit(solution)/shard_map/all_to_all | solution.py:72
  23.7 34.8 %all_gather.6 = bf16[1,1024,384]{2,1,0:T(8,128)(2,1)S(1)} all-gather(bf16[1,128,384]{2,1,0:T(8,128)(2,1)S(1)} %copy-done.3), channel_id=1, replica_groups=mesh['expert'=4,'dp'=8] {'dp'}, dimensions={1}, use_global_device_ids=true | all-gather | bytes 884736 | tf_op jit(solution)/shard_map/all_gather | solution.py:25
  59.2 3.3 %all-to-all-start.1 = ((bf16[4,12,1024]{2,1,0:T(8,128)(2,1)}), bf16[4,12,1024]{2,1,0:T(8,128)(2,1)S(1)}, u32[]{:S(2)}, u32[]{:S(2)}) async-start(bf16[4,12,1024]{2,1,0:T(8,128)(2,1)} %reshape.156), calls=%async_computation.1 | async-start | bytes 262144 | tf_op jit(solution)/shard_map/all_to_all | solution.py:65
  62.7 4.5 %all-to-all-done.1 = bf16[4,12,1024]{2,1,0:T(8,128)(2,1)S(1)} async-done(((bf16[4,12,1024]{2,1,0:T(8,128)(2,1)}), bf16[4,12,1024]{2,1,0:T(8,128)(2,1)S(1)}, u32[]{:S(2)}, u32[]{:S(2)}) %all-to-all-start.1) | async-done | bytes 98336 | tf_op jit(solution)/shard_map/all_to_all | solution.py:65
  67.1 3.3 %all-to-all-start.2 = ((bf16[4,12,1024]{2,1,0:T(8,128)(2,1)}), bf16[4,12,1024]{2,1,0:T(8,128)(2,1)S(1)}, u32[]{:S(2)}, u32[]{:S(2)}) async-start(bf16[4,12,1024]{2,1,0:T(8,128)(2,1)} %reshape.157), calls=%async_computation.2 | async-start | bytes 262144 | tf_op jit(solution)/shard_map/all_to_all | solution.py:58
  70.7 4.4 %all-to-all-done.2 = bf16[4,12,1024]{2,1,0:T(8,128)(2,1)S(1)} async-done(((bf16[4,12,1024]{2,1,0:T(8,128)(2,1)}), bf16[4,12,1024]{2,1,0:T(8,128)(2,1)S(1)}, u32[]{:S(2)}, u32[]{:S(2)}) %all-to-all-start.2) | async-done | bytes 98336 | tf_op jit(solution)/shard_map/all_to_all | solution.py:58
  75.1 1.8 %fusion.2 = f32[48,768]{1,0:T(8,128)S(1)} fusion(bf16[48,1024]{1,0:T(8,128)(2,1)S(1)} %reshape.158, bf16[1,1024,768]{2,1,0:T(8,128)(2,1)} %all-gather.2.cloned.1.call-done), kind=kOutput, calls=%fused_computation.4 | convolution fusion | flops 75497472 | bytes 1818624 | tf_op jit(solution)/shard_map/dot_general | solution.py:79
  77.1 1.6 %fusion.11 = f32[1024,384]{1,0:T(8,128)} fusion(bf16[48,384]{1,0:T(8,128)(2,1)S(1)} %get-tuple-element.57, f32[48,1024]{1,0:T(8,128)S(1)} %reshape.163, f32[48]{0:T(128)S(1)} %reshape.164), kind=kOutput, calls=%fused_computation.17 | convolution fusion | flops 37847040 | bytes 1806528 | tf_op jit(solution)/shard_map/dot_general | solution.py:11
  79.9 3.2 %all-to-all-start.4 = ((bf16[4,1,12]{2,1,0:T(2,128)(2,1)}), bf16[4,1,12]{2,1,0:T(2,128)(2,1)S(1)}, u32[]{:S(2)}, u32[]{:S(2)}) async-start(bf16[4,1,12]{2,1,0:T(2,128)(2,1)} %convert_element_type.93), calls=%async_computation.4 | async-start | bytes 4096 | tf_op jit(solution)/shard_map/all_to_all | solution.py:101
  84.4 2.4 %all-to-all-done.4 = bf16[4,1,12]{2,1,0:T(2,128)(2,1)S(1)} async-done(((bf16[4,1,12]{2,1,0:T(2,128)(2,1)}), bf16[4,1,12]{2,1,0:T(2,128)(2,1)S(1)}, u32[]{:S(2)}, u32[]{:S(2)}) %all-to-all-start.4) | async-done | bytes 128 | tf_op jit(solution)/shard_map/all_to_all | solution.py:101
  86.8 3.3 %all-to-all-start.3 = ((bf16[4,12,1024]{2,1,0:T(8,128)(2,1)}), bf16[4,12,1024]{2,1,0:T(8,128)(2,1)S(1)}, u32[]{:S(2)}, u32[]{:S(2)}) async-start(bf16[4,12,1024]{2,1,0:T(8,128)(2,1)} %reshape.159), calls=%async_computation.3 | async-start | bytes 262144 | tf_op jit(solution)/shard_map/all_to_all | solution.py:98
  90.2 0.7 fusion.30
  90.9 0.7 fusion.28
  91.7 0.7 fusion.29
  92.4 4.4 %fusion.24 = (bf16[1024]{0:T(1024)(128)(2,1)S(1)}, s32[1024,1]{0,1:T(1,128)S(1)}) fusion(bf16[]{:T(256)} %bitcast.47, bf16[]{:T(256)} %bitcast.48, bf16[]{:T(256)} %bitcast.49, bf16[]{:T(256)} %bitcast.50, bf16[]{:T(256)} %bitcast.51, bf16[]{:T(256)} %bitcast.53, bf16[]{:T(256)} %bitcast.52, pred[1024,1]{0,1:T(4,128)(4,1)S(1)} %lt.44, ...), kind=kLoop, calls=%fused_computation.93 | loop fusion | flops 18432 | bytes 15374 | tf_op jit(solution)/shard_map/gather | solution.py:108
  97.3 25.7 %select_select_fusion = bf16[1024]{0:T(1024)(128)(2,1)S(1)} fusion(pred[1024]{0:T(1024)(128)(4,1)S(1)} %get-tuple-element.52, pred[1024]{0:T(1024)(128)(4,1)S(1)} %get-tuple-element.51, pred[1024]{0:T(1024)(128)(4,1)S(1)} %get-tuple-element.50, pred[1024]{0:T(1024)(128)(4,1)S(1)} %get-tuple-element.49, pred[1024]{0:T(1024)(128)(4,1)S(1)} %get-tuple-element.48, ...), kind=kLoop, calls=%fused_computation.94 | loop fusion | flops 41984 | bytes 46162 | tf_op jit(solution)/shard_map/gather | solution.py:108
  123.8 1.0 convolution_convert_fusion
  124.9 19.4 %reduce-scatter.2.cloned.1.call-done = f32[128,384]{1,0:T(8,128)} async-done(((f32[1024,384]{1,0:T(8,128)}), f32[128,384]{1,0:T(8,128)}) %reduce-scatter.2.cloned.1.call-update) | async-done | bytes 196624 | tf_op jit(solution)/shard_map/reduce_scatter | solution.py:94
  (56 shorter events, 8.7 us)
Async XLA Ops:
  7.2 15.4 %copy-start = (bf16[128,1024]{1,0:T(8,128)(2,1)S(1)}, bf16[128,1024]{1,0:T(8,128)(2,1)}, u32[]{:S(2)}) copy-start(bf16[128,1024]{1,0:T(8,128)(2,1)} %param.7) | copy-start | bytes 786436
  7.2 16.3 %copy-start.2 = (bf16[128,1024]{1,0:T(8,128)(2,1)S(1)}, bf16[128,1024]{1,0:T(8,128)(2,1)}, u32[]{:S(2)}) copy-start(bf16[128,1024]{1,0:T(8,128)(2,1)} %param.6) | copy-start | bytes 786436
  7.2 16.6 %copy-start.3 = (bf16[1,128,384]{2,1,0:T(8,128)(2,1)S(1)}, bf16[1,128,384]{2,1,0:T(8,128)(2,1)}, u32[]{:S(2)}) copy-start(bf16[1,128,384]{2,1,0:T(8,128)(2,1)} %param.11) | copy-start | bytes 294916
  7.2 67.9 %all-gather.2.cloned.1.call-start = ((), (), s32[]{:S(2)}) async-start(), calls=%async_computation.6 | async-start | bytes 1769472 | tf_op jit(solution)/shard_map/all_gather | solution.py:24
  18.3 40.9 %all-to-all-start = ((bf16[4,1,12]{2,1,0:T(2,128)(2,1)}), bf16[4,1,12]{2,1,0:T(2,128)(2,1)S(1)}, u32[]{:S(2)}, u32[]{:S(2)}) async-start(bf16[4,1,12]{2,1,0:T(2,128)(2,1)} %all_to_all.25), calls=%async_computation | async-start | bytes 4096 | tf_op jit(solution)/shard_map/all_to_all | solution.py:72
  59.2 7.9 %all-to-all-start.1 = ((bf16[4,12,1024]{2,1,0:T(8,128)(2,1)}), bf16[4,12,1024]{2,1,0:T(8,128)(2,1)S(1)}, u32[]{:S(2)}, u32[]{:S(2)}) async-start(bf16[4,12,1024]{2,1,0:T(8,128)(2,1)} %reshape.156), calls=%async_computation.1 | async-start | bytes 262144 | tf_op jit(solution)/shard_map/all_to_all | solution.py:65
  67.1 7.9 %all-to-all-start.2 = ((bf16[4,12,1024]{2,1,0:T(8,128)(2,1)}), bf16[4,12,1024]{2,1,0:T(8,128)(2,1)S(1)}, u32[]{:S(2)}, u32[]{:S(2)}) async-start(bf16[4,12,1024]{2,1,0:T(8,128)(2,1)} %reshape.157), calls=%async_computation.2 | async-start | bytes 262144 | tf_op jit(solution)/shard_map/all_to_all | solution.py:58
  70.5 73.8 %reduce-scatter.2.cloned.1.call-start = ((), (), s32[]{:S(2)}) async-start(), calls=%async_computation.7 | async-start | bytes 1769472 | tf_op jit(solution)/shard_map/reduce_scatter | solution.py:94
  78.7 4.4 %copy-start.1 = (bf16[1,1024,768]{2,1,0:T(8,128)(2,1)S(1)}, bf16[1,1024,768]{2,1,0:T(8,128)(2,1)}, u32[]{:S(2)}) copy-start(bf16[1,1024,768]{2,1,0:T(8,128)(2,1)} %all-gather.2.cloned.1.call-done) | copy-start | bytes 4718596
  79.9 6.9 %all-to-all-start.4 = ((bf16[4,1,12]{2,1,0:T(2,128)(2,1)}), bf16[4,1,12]{2,1,0:T(2,128)(2,1)S(1)}, u32[]{:S(2)}, u32[]{:S(2)}) async-start(bf16[4,1,12]{2,1,0:T(2,128)(2,1)} %convert_element_type.93), calls=%async_computation.4 | async-start | bytes 4096 | tf_op jit(solution)/shard_map/all_to_all | solution.py:101
  86.8 37.0 %all-to-all-start.3 = ((bf16[4,12,1024]{2,1,0:T(8,128)(2,1)}), bf16[4,12,1024]{2,1,0:T(8,128)(2,1)S(1)}, u32[]{:S(2)}, u32[]{:S(2)}) async-start(bf16[4,12,1024]{2,1,0:T(8,128)(2,1)} %reshape.159), calls=%async_computation.3 | async-start | bytes 262144 | tf_op jit(solution)/shard_map/all_to_all | solution.py:98
Sparse Core Ops, SparseCore 0:
  10.2 53.8 all-gather.1
  78.9 65.3 reduce-scatter.1
where the time goes:
time: 152 us; the launch traced here: 151 us
  blocking collectives  34.8 us (23%)
  other arithmetic  32.9 us (22%)
  waiting for transfers between devices  31.3 us (21%)
  starting transfers between devices  17.5 us (12%)
  between operations  14.3 us (9%)
  local copies, waits for them, and re-layouts  14.1 us (9%)
  matrix products  6.16 us (4%)
    all_gather x1, blocking collectives, on_device(): lax.all_gather(down_w, 'dp', axis=1, tiled=True)  34.8 us
    gather x3, other arithmetic, on_device(): gathered_grads = back_grads[jnp.minimum(slot_of, slot_count - 1)]  30.6 us
    reduce_scatter x1, waiting for transfers between devices, on_device(): lax.psum_scatter(transpose_product(d_expert_out, hidden), 'dp', scatter_d...  19.4 us
    all_to_all x1, waiting for transfers between devices, on_device(): lax.all_to_all(send_upstream.reshape(groups, CAP, features), 'expert', sp...  4.46 us
    all_to_all x1, waiting for transfers between devices, on_device(): lax.all_to_all(send_inputs.reshape(groups, CAP, features), 'expert', spli...  4.36 us
    scatter x1, local copies, waits for them, and re-layouts, on_device(): owner = jnp.full((slot_count,), -1, jnp.int32).at[slot_of].set(jnp.arange...  4.3 us
    all_to_all x1, starting transfers between devices, on_device(): lax.all_to_all(send_gates.reshape(groups, CAP), 'expert', split_axis=0, c...  4.26 us
    all_to_all x1, starting transfers between devices, on_device(): lax.all_to_all(send_upstream.reshape(groups, CAP, features), 'expert', sp...  3.33 us
  transfers between devices with their start and end apart: 7, of which 4 were waited for; matrix products, arithmetic and copies ran while one was open for 32% of the time, Pallas kernels for 0%

commit v1 on v0

--- a/solution.py
+++ b/solution.py
@@ -5,6 +5,28 @@
 
 TOPK = 8
 CAP = 12
+
+
+def split_up(array, dim, devices):
+    before, after = (array.shape[:dim], array.shape[dim + 1 :])
+    return jnp.moveaxis(array.reshape(*before, devices, -1, *after), dim, 0)
+
+
+def laid_out(blocks, dim):
+    blocks = jnp.moveaxis(blocks, 0, dim)
+    dims = blocks.shape
+    return blocks.reshape(*dims[:dim], dims[dim] * dims[dim + 1], *dims[dim + 2 :])
+
+
+def exchange_directly(value, axis, split_dim, concat_dim):
+    peers, index = (lax.axis_size(axis), lax.axis_index(axis))
+    tiles = split_up(value, split_dim, peers)
+    outs = [tiles[index]]
+    for turn in range(1, peers):
+        sent = tiles[(index + turn) % peers]
+        outs.append(lax.ppermute(sent, axis, [(i, (i + turn) % peers) for i in range(peers)]))
+    tiles = jnp.stack(outs)[(index - jnp.arange(peers)) % peers]
+    return laid_out(tiles, concat_dim)
 
 
 def transpose_product(left, right):
@@ -62,13 +84,7 @@
             concat_axis=0,
             tiled=True,
         ),
-        lax.all_to_all(
-            send_upstream.reshape(groups, CAP, features),
-            "expert",
-            split_axis=0,
-            concat_axis=0,
-            tiled=True,
-        ),
+        exchange_directly(send_upstream.reshape(groups, CAP, features), "expert", 0, 0),
         lax.all_to_all(
             send_gates.reshape(groups, CAP), "expert", split_axis=0, concat_axis=0, tiled=True
         ),

time: 152 us -> 146 us (0.961)
  waiting for transfers between devices: 31.3 us -> 26.7 us
    all_to_all x1 -> x0, waiting for transfers between devices: 4.46 us -> none  [on_device(): lax.all_to_all(send_upstream.reshape(groups, CAP, features), 'expert', sp...]
    all_to_all x1 -> x0, starting transfers between devices: 3.33 us -> none  [on_device(): lax.all_to_all(send_upstream.reshape(groups, CAP, features), 'expert', sp...]
    ppermute x0 -> x3, starting transfers between devices: none -> 2.31 us  [exchange_directly(): lax.ppermute(sent, axis, [(i, (i + turn) % peers) for i in range(peers)])]
  transfers between devices with their start and end apart: 7 -> 9, of which waited for: 4 -> 3; matrix products, arithmetic and copies ran while one was open for 32% -> 34% of each run, Pallas kernels for 0% -> 0%
where the time goes in v1:
time: 146 us; the launch traced here: 145 us
  blocking collectives  34.3 us (23%)
  other arithmetic  33 us (23%)
  waiting for transfers between devices  26.7 us (18%)
  starting transfers between devices  16.5 us (11%)
  between operations  14.4 us (10%)
  local copies, waits for them, and re-layouts  14 us (10%)
  matrix products  6.16 us (4%)
    all_gather x1, blocking collectives, on_device(): lax.all_gather(down_w, 'dp', axis=1, tiled=True)  34.3 us
    gather x3, other arithmetic, on_device(): gathered_grads = back_grads[jnp.minimum(slot_of, slot_count - 1)]  30.6 us
    reduce_scatter x1, waiting for transfers between devices, on_device(): lax.psum_scatter(transpose_product(d_expert_out, hidden), 'dp', scatter_d...  20 us
    scatter x1, local copies, waits for them, and re-layouts, on_device(): owner = jnp.full((slot_count,), -1, jnp.int32).at[slot_of].set(jnp.arange...  4.3 us
    all_to_all x1, starting transfers between devices, on_device(): lax.all_to_all(send_gates.reshape(groups, CAP), 'expert', split_axis=0, c...  4.26 us
    all_to_all x1, waiting for transfers between devices, on_device(): lax.all_to_all(send_inputs.reshape(groups, CAP, features), 'expert', spli...  3.63 us
    all_to_all x1, starting transfers between devices, on_device(): lax.all_to_all(send_inputs.reshape(groups, CAP, features), 'expert', spli...  3.33 us
    all_to_all x1, starting transfers between devices, on_device(): lax.all_to_all(d_slot.reshape(groups, CAP, features), 'expert', split_axi...  3.33 us
  transfers between devices with their start and end apart: 9, of which 3 were waited for; matrix products, arithmetic and copies ran while one was open for 34% of the time, Pallas kernels for 0%

profile of v1, /device:TPU:0, one launch (start us, length us, event | category | flops | bytes accessed | tf_op | source)
XLA Modules:
  0.0 145.0 jit_solution(13455578409143588761)
XLA Ops:
  7.2 0.7 all-gather.2.cloned.1.call-update
  7.9 0.8 copy.23
  8.7 0.7 broadcast_multiply_fusion
  9.5 1.1 reduce-window.6
  11.5 0.8 copy.27
  12.5 4.3 %scatter_custom_fusion = s32[48]{0:T(128)S(1)} fusion(s32[1024]{0:T(1024)S(1)} %bitcast.118, s32[1024]{0:T(1024)S(1)} %iota.19, s32[]{:T(128)} %constant.67.clone.1), kind=kCustom, calls=%fused_computation.114 | custom fusion | bytes 196 | tf_op jit(solution)/shard_map/scatter | solution.py:66
  16.9 0.8 gather_fusion
  18.3 4.3 %all-to-all-start = ((bf16[4,1,12]{2,1,0:T(2,128)(2,1)}), bf16[4,1,12]{2,1,0:T(2,128)(2,1)S(1)}, u32[]{:S(2)}, u32[]{:S(2)}) async-start(bf16[4,1,12]{2,1,0:T(2,128)(2,1)} %all_to_all.21), calls=%async_computation | async-start | bytes 4096 | tf_op jit(solution)/shard_map/all_to_all | solution.py:88
  22.9 1.8 %collective-permute-start.2 = (bf16[1,12,1024]{2,1,0:T(8,128)(2,1)S(1)}, bf16[1,12,1024]{2,1,0:T(8,128)(2,1)S(1)}, u32[]{:S(2)}, u32[]{:S(2)}) collective-permute-start(bf16[1,12,1024]{2,1,0:T(8,128)(2,1)S(1)} %get-tuple-element.59), channel_id=1, source_target_pairs={{0,24},{8,0},{16,8},{24,16},{1,25},{9,1},{17,9},{25,17},{2,26},{10... | collective-permute-start | bytes 73736 | tf_op jit(solution)/shard_map/ppermute | solution.py:27
  25.5 34.3 %all_gather.6 = bf16[1,1024,384]{2,1,0:T(8,128)(2,1)S(1)} all-gather(bf16[1,128,384]{2,1,0:T(8,128)(2,1)S(1)} %copy-done.3), channel_id=1, replica_groups=mesh['expert'=4,'dp'=8] {'dp'}, dimensions={1}, use_global_device_ids=true | all-gather | bytes 884736 | tf_op jit(solution)/shard_map/all_gather | solution.py:47
  60.5 3.3 %all-to-all-start.1 = ((bf16[4,12,1024]{2,1,0:T(8,128)(2,1)}), bf16[4,12,1024]{2,1,0:T(8,128)(2,1)S(1)}, u32[]{:S(2)}, u32[]{:S(2)}) async-start(bf16[4,12,1024]{2,1,0:T(8,128)(2,1)} %reshape.242), calls=%async_computation.1 | async-start | bytes 262144 | tf_op jit(solution)/shard_map/all_to_all | solution.py:80
  64.8 3.6 %all-to-all-done.1 = bf16[4,12,1024]{2,1,0:T(8,128)(2,1)S(1)} async-done(((bf16[4,12,1024]{2,1,0:T(8,128)(2,1)}), bf16[4,12,1024]{2,1,0:T(8,128)(2,1)S(1)}, u32[]{:S(2)}, u32[]{:S(2)}) %all-to-all-start.1) | async-done | bytes 98336 | tf_op jit(solution)/shard_map/all_to_all | solution.py:80
  68.5 1.8 %fusion.2 = f32[48,768]{1,0:T(8,128)S(1)} fusion(bf16[48,1024]{1,0:T(8,128)(2,1)S(1)} %reshape.243, bf16[1,1024,768]{2,1,0:T(8,128)(2,1)} %all-gather.2.cloned.1.call-done), kind=kOutput, calls=%fused_computation.5 | convolution fusion | flops 75497472 | bytes 1818624 | tf_op jit(solution)/shard_map/dot_general | solution.py:95
  70.5 1.6 %fusion.12 = f32[1024,384]{1,0:T(8,128)} fusion(bf16[48,384]{1,0:T(8,128)(2,1)S(1)} %get-tuple-element.57, f32[48,1024]{1,0:T(8,128)S(1)} %reshape.248, f32[48]{0:T(128)S(1)} %reshape.249), kind=kOutput, calls=%fused_computation.20 | convolution fusion | flops 37847040 | bytes 1806528 | tf_op jit(solution)/shard_map/dot_general | solution.py:33
  73.3 3.2 %all-to-all-start.3 = ((bf16[4,1,12]{2,1,0:T(2,128)(2,1)}), bf16[4,1,12]{2,1,0:T(2,128)(2,1)S(1)}, u32[]{:S(2)}, u32[]{:S(2)}) async-start(bf16[4,1,12]{2,1,0:T(2,128)(2,1)} %convert_element_type.119), calls=%async_computation.3 | async-start | bytes 4096 | tf_op jit(solution)/shard_map/all_to_all | solution.py:117
  77.8 2.4 %all-to-all-done.3 = bf16[4,1,12]{2,1,0:T(2,128)(2,1)S(1)} async-done(((bf16[4,1,12]{2,1,0:T(2,128)(2,1)}), bf16[4,1,12]{2,1,0:T(2,128)(2,1)S(1)}, u32[]{:S(2)}, u32[]{:S(2)}) %all-to-all-start.3) | async-done | bytes 128 | tf_op jit(solution)/shard_map/all_to_all | solution.py:117
  80.2 3.3 %all-to-all-start.2 = ((bf16[4,12,1024]{2,1,0:T(8,128)(2,1)}), bf16[4,12,1024]{2,1,0:T(8,128)(2,1)S(1)}, u32[]{:S(2)}, u32[]{:S(2)}) async-start(bf16[4,12,1024]{2,1,0:T(8,128)(2,1)} %reshape.244), calls=%async_computation.2 | async-start | bytes 262144 | tf_op jit(solution)/shard_map/all_to_all | solution.py:114
  83.6 0.7 fusion.33
  84.3 0.7 fusion.31
  85.0 0.7 fusion.32
  85.8 4.4 %fusion.25 = (bf16[1024]{0:T(1024)(128)(2,1)S(1)}, s32[1024,1]{0,1:T(1,128)S(1)}) fusion(bf16[]{:T(256)} %bitcast.56, bf16[]{:T(256)} %bitcast.57, bf16[]{:T(256)} %bitcast.58, bf16[]{:T(256)} %bitcast.59, bf16[]{:T(256)} %bitcast.60, bf16[]{:T(256)} %bitcast.62, bf16[]{:T(256)} %bitcast.61, pred[1024,1]{0,1:T(4,128)(4,1)S(1)} %lt.86, ...), kind=kLoop, calls=%fused_computation.100 | loop fusion | flops 18432 | bytes 15374 | tf_op jit(solution)/shard_map/gather | solution.py:124
  90.7 25.7 %select_select_fusion = bf16[1024]{0:T(1024)(128)(2,1)S(1)} fusion(pred[1024]{0:T(1024)(128)(4,1)S(1)} %get-tuple-element.52, pred[1024]{0:T(1024)(128)(4,1)S(1)} %get-tuple-element.51, pred[1024]{0:T(1024)(128)(4,1)S(1)} %get-tuple-element.50, pred[1024]{0:T(1024)(128)(4,1)S(1)} %get-tuple-element.49, pred[1024]{0:T(1024)(128)(4,1)S(1)} %get-tuple-element.48, ...), kind=kLoop, calls=%fused_computation.104 | loop fusion | flops 41984 | bytes 46162 | tf_op jit(solution)/shard_map/gather | solution.py:124
  117.2 1.0 convolution_convert_fusion
  118.2 20.0 %reduce-scatter.2.cloned.1.call-done = f32[128,384]{1,0:T(8,128)} async-done(((f32[1024,384]{1,0:T(8,128)}), f32[128,384]{1,0:T(8,128)}) %reduce-scatter.2.cloned.1.call-update) | async-done | bytes 196624 | tf_op jit(solution)/shard_map/reduce_scatter | solution.py:110
  (65 shorter events, 8.5 us)
Async XLA Ops:
  7.2 15.4 %copy-start = (bf16[128,1024]{1,0:T(8,128)(2,1)S(1)}, bf16[128,1024]{1,0:T(8,128)(2,1)}, u32[]{:S(2)}) copy-start(bf16[128,1024]{1,0:T(8,128)(2,1)} %param.7) | copy-start | bytes 786436
  7.2 18.1 %copy-start.2 = (bf16[128,1024]{1,0:T(8,128)(2,1)S(1)}, bf16[128,1024]{1,0:T(8,128)(2,1)}, u32[]{:S(2)}) copy-start(bf16[128,1024]{1,0:T(8,128)(2,1)} %param.6) | copy-start | bytes 786436
  7.2 18.3 %copy-start.3 = (bf16[1,128,384]{2,1,0:T(8,128)(2,1)S(1)}, bf16[1,128,384]{2,1,0:T(8,128)(2,1)}, u32[]{:S(2)}) copy-start(bf16[1,128,384]{2,1,0:T(8,128)(2,1)} %param.11) | copy-start | bytes 294916
  7.2 61.2 %all-gather.2.cloned.1.call-start = ((), (), s32[]{:S(2)}) async-start(), calls=%async_computation.5 | async-start | bytes 1769472 | tf_op jit(solution)/shard_map/all_gather | solution.py:46
  18.3 42.2 %all-to-all-start = ((bf16[4,1,12]{2,1,0:T(2,128)(2,1)}), bf16[4,1,12]{2,1,0:T(2,128)(2,1)S(1)}, u32[]{:S(2)}, u32[]{:S(2)}) async-start(bf16[4,1,12]{2,1,0:T(2,128)(2,1)} %all_to_all.21), calls=%async_computation | async-start | bytes 4096 | tf_op jit(solution)/shard_map/all_to_all | solution.py:88
  22.9 41.1 %collective-permute-start.2 = (bf16[1,12,1024]{2,1,0:T(8,128)(2,1)S(1)}, bf16[1,12,1024]{2,1,0:T(8,128)(2,1)S(1)}, u32[]{:S(2)}, u32[]{:S(2)}) collective-permute-start(bf16[1,12,1024]{2,1,0:T(8,128)(2,1)S(1)} %get-tuple-element.59), channel_id=1, source_target_pairs={{0,24},{8,0},{16,8},{24,16},{1,25},{9,1},{17,9},{25,17},{2,26},{10... | collective-permute-start | bytes 73736 | tf_op jit(solution)/shard_map/ppermute | solution.py:27
  24.7 39.3 %collective-permute-start.1 = (bf16[1,12,1024]{2,1,0:T(8,128)(2,1)S(1)}, bf16[1,12,1024]{2,1,0:T(8,128)(2,1)S(1)}, u32[]{:S(2)}, u32[]{:S(2)}) collective-permute-start(bf16[1,12,1024]{2,1,0:T(8,128)(2,1)S(1)} %get-tuple-element.60), channel_id=1, source_target_pairs={{0,16},{8,24},{16,0},{24,8},{1,17},{9,25},{17,1},{25,9},{2,18},{10... | collective-permute-start | bytes 73736 | tf_op jit(solution)/shard_map/ppermute | solution.py:27
  25.1 38.9 %collective-permute-start = (bf16[1,12,1024]{2,1,0:T(8,128)(2,1)S(1)}, bf16[1,12,1024]{2,1,0:T(8,128)(2,1)S(1)}, u32[]{:S(2)}, u32[]{:S(2)}) collective-permute-start(bf16[1,12,1024]{2,1,0:T(8,128)(2,1)S(1)} %get-tuple-element.61), channel_id=1, source_target_pairs={{0,8},{8,16},{16,24},{24,0},{1,9},{9,17},{17,25},{25,1},{2,10},{10... | collective-permute-start | bytes 73736 | tf_op jit(solution)/shard_map/ppermute | solution.py:27
  60.5 7.9 %all-to-all-start.1 = ((bf16[4,12,1024]{2,1,0:T(8,128)(2,1)}), bf16[4,12,1024]{2,1,0:T(8,128)(2,1)S(1)}, u32[]{:S(2)}, u32[]{:S(2)}) async-start(bf16[4,12,1024]{2,1,0:T(8,128)(2,1)} %reshape.242), calls=%async_computation.1 | async-start | bytes 262144 | tf_op jit(solution)/shard_map/all_to_all | solution.py:80
  63.8 74.4 %reduce-scatter.2.cloned.1.call-start = ((), (), s32[]{:S(2)}) async-start(), calls=%async_computation.6 | async-start | bytes 1769472 | tf_op jit(solution)/shard_map/reduce_scatter | solution.py:110
  72.1 4.4 %copy-start.1 = (bf16[1,1024,768]{2,1,0:T(8,128)(2,1)S(1)}, bf16[1,1024,768]{2,1,0:T(8,128)(2,1)}, u32[]{:S(2)}) copy-start(bf16[1,1024,768]{2,1,0:T(8,128)(2,1)} %all-gather.2.cloned.1.call-done) | copy-start | bytes 4718596
  73.3 6.9 %all-to-all-start.3 = ((bf16[4,1,12]{2,1,0:T(2,128)(2,1)}), bf16[4,1,12]{2,1,0:T(2,128)(2,1)S(1)}, u32[]{:S(2)}, u32[]{:S(2)}) async-start(bf16[4,1,12]{2,1,0:T(2,128)(2,1)} %convert_element_type.119), calls=%async_computation.3 | async-start | bytes 4096 | tf_op jit(solution)/shard_map/all_to_all | solution.py:117
  80.2 37.0 %all-to-all-start.2 = ((bf16[4,12,1024]{2,1,0:T(8,128)(2,1)}), bf16[4,12,1024]{2,1,0:T(8,128)(2,1)S(1)}, u32[]{:S(2)}, u32[]{:S(2)}) async-start(bf16[4,12,1024]{2,1,0:T(8,128)(2,1)} %reshape.244), calls=%async_computation.2 | async-start | bytes 262144 | tf_op jit(solution)/shard_map/all_to_all | solution.py:114
Sparse Core Ops, SparseCore 0:
  10.2 55.0 all-gather.1
  72.3 65.8 reduce-scatter.1
